TPU v7x, 32 devices: a whole 2x2x4 slice. The times are simulated.
32 devices in a mesh: fsdp: 16 (over z, y, core), ctx: 2 (over x).
Axes of the slice: x: 2, y: 2, z: 4, core: 2. Of those that a mesh axis runs over, the one named last changes fastest.
Arguments:
- q_nope: bfloat16 [16, 256, 1024], P('fsdp', 'ctx'), may hold values from -6 to 6
- q_rope: bfloat16 [16, 256, 512], P('fsdp', 'ctx'), may hold values from -450 to 450
- kv_latent: bfloat16 [16, 256, 512], P('fsdp', 'ctx'), may hold values from -6 to 6
- key_rope: bfloat16 [16, 256, 64], P('fsdp', 'ctx'), may hold values from -6 to 6
- weight_codes: bfloat16 [512, 2048], P('fsdp'), may hold values from -0.25 to 0.25
- exponents: int32 [4, 16], replicated, may hold values from -1 to 1
- doc_ids: int32 [16, 256], P('fsdp'), may hold values from 0 to 3, never falling along the last dimension, each value on 1 to 128 neighbouring positions
Outputs:
- scaled_out: bfloat16 [16, 256, 1024], P('fsdp', 'ctx')
Inputs may be any that keep to these rules, and one draw needn't show every extreme that they name: `doc_ids`: each document of a sequence covers consecutive positions, at most 128 of them.
All inputs are finite; a program needn't handle non-finite values. Where the computation divides by a largest or mean magnitude, that divisor is 1e-20 or more.
Results may differ from a plain program's by a relative error of at most 0.0085.
Values may be sent and summed in bfloat16 or wider, within the bound.
A program may use at most 64 MiB of HBM per device.

v0:
```python
import jax
import jax.numpy as jnp
from jax import lax
from jax.sharding import PartitionSpec as P

DN = 128
DR = 64
DV = 128
BLK = 128


def dequantize(codes, exponents):
    nrow, ncol = exponents.shape
    factor = jnp.exp2(exponents.astype(jnp.float32)).astype(jnp.bfloat16)
    scaled = codes.reshape(nrow, BLK, ncol, BLK) * factor[:, None, :, None]
    return scaled.reshape(codes.shape)


def attend(queries, rotary, keys_values, rope_all, query_places, query_docs, docs):
    length = keys_values.shape[0]
    k_nope = keys_values[:, :, :DN]
    values = keys_values[:, :, DN:]
    scores = jnp.einsum("qhd,khd->hqk", queries, k_nope, preferred_element_type=jnp.float32)
    scores = scores + jnp.einsum(
        "qhd,kd->hqk", rotary, rope_all, preferred_element_type=jnp.float32
    )
    scores = scores * (DN + DR) ** (-0.5)
    key_places = jnp.arange(length, dtype=jnp.int32)
    allowed = (key_places[None, :] <= query_places[:, None]) & (
        docs[None, :] == query_docs[:, None]
    )
    scores = jnp.where(allowed[None], scores, jnp.float32(-1e30))
    top = jnp.max(scores, axis=-1, keepdims=True)
    expo = jnp.exp(scores - top)
    probs = (expo / jnp.sum(expo, axis=-1, keepdims=True)).astype(jnp.bfloat16)
    return jnp.einsum("hqk,khd->qhd", probs, values, preferred_element_type=jnp.float32)


def per_device(q_nope, q_rope, kv_latent, key_rope, weight_codes, exponents, doc_ids):
    tok = q_nope.shape[1]
    heads = q_nope.shape[2] // DN
    groups = lax.axis_size("ctx")
    length = tok * groups
    offset = lax.axis_index("ctx") * tok
    docs = doc_ids[0]
    latent_all, rope_all = (
        lax.all_gather(kv_latent[0], "ctx", axis=0, tiled=True),
        lax.all_gather(key_rope[0], "ctx", axis=0, tiled=True),
    )
    codes = lax.all_gather(weight_codes, "fsdp", axis=0, tiled=True)
    weight = dequantize(codes, exponents)
    keys_values = jnp.dot(latent_all, weight, preferred_element_type=jnp.float32).astype(
        jnp.bfloat16
    )
    keys_values = keys_values.reshape(length, heads, DN + DV)
    queries = q_nope[0].reshape(tok, heads, DN)
    rotary = q_rope[0].reshape(tok, heads, DR)
    query_docs = lax.dynamic_slice_in_dim(docs, offset, tok)
    query_places = offset + jnp.arange(tok, dtype=jnp.int32)
    attended = attend(queries, rotary, keys_values, rope_all, query_places, query_docs, docs)
    attended = attended.reshape(tok, heads * DV)
    amax = lax.pmax(jnp.max(jnp.abs(attended)), ("fsdp", "ctx"))
    return (attended / amax).reshape(1, tok, heads * DV).astype(jnp.bfloat16)


def solution(mesh):
    in_specs = (
        P("fsdp", "ctx", None),
        P("fsdp", "ctx", None),
        P("fsdp", "ctx", None),
        P("fsdp", "ctx", None),
        P("fsdp", None),
        P(),
        P("fsdp", None),
    )
    out_specs = P("fsdp", "ctx", None)
    return jax.shard_map(
        per_device, mesh=mesh, in_specs=in_specs, out_specs=out_specs, check_vma=False
    )
```

profile of v0, /device:TPU:0, one launch (start us, length us, event | category | flops | bytes accessed | tf_op | source)
XLA Modules:
  0.0 105.1 jit_solution(8917940227443522955)
XLA Ops:
  6.5 0.0 all-gather.4.cloned.1.call-start
  6.5 0.7 all-gather.4.cloned.1.call-update
  7.3 1.0 copy.21
  8.3 1.0 copy.15
  9.3 5.6 %all-gather.1 = bf16[1,256,64]{1,2,0:T(8,128)(2,1)S(1)} all-gather(bf16[1,128,64]{1,2,0:T(8,128)(2,1)} %param.10), channel_id=3, replica_groups=mesh['fsdp'=16,'ctx'=2] {'ctx'}, dimensions={1}, use_global_device_ids=true | all-gather | bytes 49152 | tf_op jit(solution)/shard_map/all_gather | solution.py:48
  14.9 5.8 %all-gather = bf16[1,256,512]{2,1,0:T(8,128)(2,1)S(1)} all-gather(bf16[1,128,512]{2,1,0:T(8,128)(2,1)} %param.9), channel_id=2, replica_groups=mesh['fsdp'=16,'ctx'=2] {'ctx'}, dimensions={1}, use_global_device_ids=true | all-gather | bytes 393216 | tf_op jit(solution)/shard_map/all_gather | solution.py:47
  20.8 0.7 dynamic-slice_bitcast_fusion
  21.4 0.7 exponential_convert_fusion
  22.1 0.8 fusion.12
  22.9 30.8 %all-gather.4.cloned.1.call-done = bf16[512,2048]{1,0:T(8,128)(2,1)} async-done(((bf16[32,2048]{1,0:T(8,128)(2,1)}), bf16[512,2048]{1,0:T(8,128)(2,1)}) %all-gather.4.cloned.1.call-update) | async-done | bytes 2097168 | tf_op jit(solution)/shard_map/all_gather | solution.py:50
  53.7 0.0 copy-start
  53.7 0.3 mul.20
  54.1 1.2 %copy-done = bf16[512,2048]{1,0:T(8,128)(2,1)S(1)} copy-done((bf16[512,2048]{1,0:T(8,128)(2,1)S(1)}, bf16[512,2048]{1,0:T(8,128)(2,1)}, u32[]{:S(2)}) %copy-start) | copy-done | bytes 2097176
  55.3 1.2 %convolution_convert_fusion = bf16[2048,256]{1,0:T(8,128)(2,1)S(1)} fusion(bf16[512,2048]{1,0:T(8,128)(2,1)S(1)} %copy-done, bf16[64,8,16,128]{3,2,1,0:T(8,128)(2,1)S(1)} %bitcast.38, bf16[1,256,512]{2,1,0:T(8,128)(2,1)S(1)} %all-gather), kind=kOutput, calls=%fused_computation.1 | convolution fusion | flops 538443776 | bytes 5505024 | tf_op jit(solution)/shard_map/dot_general | solution.py:52
  56.5 0.3 convolution_bitcast_fusion.1
  56.9 0.3 fusion.6
  57.2 0.2 fusion.15
  57.5 1.0 abs_reduce_fusion
  58.5 38.2 %pmax.7 = f32[]{:T(128)} all-reduce(f32[]{:T(128)} %get-tuple-element.5), channel_id=1, replica_groups=mesh['fsdp'=16,'ctx'=2] {'fsdp','ctx'}, use_global_device_ids=true, to_apply=%region_3.4 | all-reduce | flops 1 | bytes 8 | tf_op jit(solution)/shard_map/pmax | solution.py:62
  96.7 0.7 divide_convert_fusion.1
  97.4 0.9 copy.17
  (1 shorter events, 0.0 us)
Async XLA Ops:
  6.5 47.2 %all-gather.4.cloned.1.call-start = ((), (), s32[]{:S(2)}) async-start(), calls=%async_computation | async-start | bytes 2228224 | tf_op jit(solution)/shard_map/all_gather | solution.py:50
  53.7 1.6 %copy-start = (bf16[512,2048]{1,0:T(8,128)(2,1)S(1)}, bf16[512,2048]{1,0:T(8,128)(2,1)}, u32[]{:S(2)}) copy-start(bf16[512,2048]{1,0:T(8,128)(2,1)} %all-gather.4.cloned.1.call-done) | copy-start | bytes 6291460
Sparse Core Ops, SparseCore 0:
  9.5 44.1 all-gather.3
where the time goes:
time: 105 us
  blocking collectives  49.7 us (47%)
  waiting for transfers between devices  31.5 us (30%)
  between operations  13.5 us (13%)
  local copies, waits for them, and re-layouts  5.1 us (5%)
  matrix products  2.96 us (3%)
  other arithmetic  2.4 us (2%)
    pmax x1, blocking collectives, per_device(): amax = lax.pmax(jnp.max(jnp.abs(attended)), ('fsdp', 'ctx'))  38.2 us
    all_gather x1, waiting for transfers between devices, per_device(): codes = lax.all_gather(weight_codes, 'fsdp', axis=0, tiled=True)  30.8 us
    all_gather x1, blocking collectives, per_device(): lax.all_gather(kv_latent[0], 'ctx', axis=0, tiled=True)  5.84 us
    all_gather x1, blocking collectives, per_device(): lax.all_gather(key_rope[0], 'ctx', axis=0, tiled=True)  5.64 us
    unnamed x4, local copies, waits for them, and re-layouts  3.26 us
  transfers between devices with their start and end apart: 1, of which 1 were waited for; matrix products, arithmetic and copies ran while one was open for 4% of the time, Pallas kernels for 0%

commit v1 on v0

--- a/solution.py
+++ b/solution.py
@@ -7,6 +7,17 @@
 DR = 64
 DV = 128
 BLK = 128
+
+
+def around_the_ring(shard, axis, dim):
+    size = lax.axis_size(axis)
+    hops = [(i, (i + 1) % size) for i in range(size)]
+    parts = [shard]
+    for far in range(1, size):
+        parts = [lax.ppermute(parts[0], axis, hops), *parts]
+    whole = jnp.concatenate(parts, axis=dim)
+    shift = (lax.axis_index(axis) + 1) * parts[-1].shape[dim]
+    return jnp.roll(whole, shift, axis=dim)
 
 
 def dequantize(codes, exponents):
@@ -47,7 +58,7 @@
         lax.all_gather(kv_latent[0], "ctx", axis=0, tiled=True),
         lax.all_gather(key_rope[0], "ctx", axis=0, tiled=True),
     )
-    codes = lax.all_gather(weight_codes, "fsdp", axis=0, tiled=True)
+    codes = around_the_ring(weight_codes, "fsdp", 0)
     weight = dequantize(codes, exponents)
     keys_values = jnp.dot(latent_all, weight, preferred_element_type=jnp.float32).astype(
         jnp.bfloat16

time: 105 us -> 159 us (1.51); the launches traced: 105 us -> 157 us
  waiting for transfers between devices: 31.5 us -> 98.6 us
  between operations: 13.5 us -> 0.34 us
  blocking collectives: 49.7 us -> 47.5 us
    ppermute x0 -> x15, waiting for transfers between devices: none -> 98.6 us  [around_the_ring(): parts = [lax.ppermute(parts[0], axis, hops), *parts]]
    all_gather x1 -> x0, waiting for transfers between devices: 30.8 us -> none  [per_device(): codes = lax.all_gather(weight_codes, 'fsdp', axis=0, tiled=True)]
    unnamed x4 -> x35, local copies, waits for them, and re-layouts: 3.26 us -> 2.36 us
  transfers between devices with their start and end apart: 1 -> 15, of which waited for: 1 -> 14; matrix products, arithmetic and copies ran while one was open for 4% -> 3% of each run, Pallas kernels for 0% -> 0%
where the time goes in v1:
time: 159 us; the launch traced here: 157 us
  waiting for transfers between devices  98.6 us (62%)
  blocking collectives  47.5 us (30%)
  local copies, waits for them, and re-layouts  4.22 us (3%)
  matrix products  3.55 us (2%)
  other arithmetic  2.4 us (2%)
    ppermute x15, waiting for transfers between devices, around_the_ring(): parts = [lax.ppermute(parts[0], axis, hops), *parts]  98.6 us
    pmax x1, blocking collectives, per_device(): amax = lax.pmax(jnp.max(jnp.abs(attended)), ('fsdp', 'ctx'))  37 us
    all_gather x1, blocking collectives, per_device(): lax.all_gather(kv_latent[0], 'ctx', axis=0, tiled=True)  5.84 us
    all_gather x1, blocking collectives, per_device(): lax.all_gather(key_rope[0], 'ctx', axis=0, tiled=True)  4.65 us
  transfers between devices with their start and end apart: 15, of which 14 were waited for; matrix products, arithmetic and copies ran while one was open for 3% of the time, Pallas kernels for 0%

profile of v1, /device:TPU:0, one launch (start us, length us, event | category | flops | bytes accessed | tf_op | source)
XLA Modules:
  0.0 157.1 jit_solution(8313681566779227571)
XLA Ops:
  0.0 0.5 collective-permute-start
  0.5 7.9 %collective-permute-done = bf16[32,2048]{1,0:T(8,128)(2,1)S(1)} collective-permute-done((bf16[32,2048]{1,0:T(8,128)(2,1)}, bf16[32,2048]{1,0:T(8,128)(2,1)S(1)}, u32[]{:S(2)}, u32[]{:S(2)}) %collective-permute-start) | collective-permute-done | bytes 131104 | tf_op jit(solution)/shard_map/ppermute | solution.py:17
  8.4 7.1 %collective-permute-done.1 = bf16[32,2048]{1,0:T(8,128)(2,1)S(1)} collective-permute-done((bf16[32,2048]{1,0:T(8,128)(2,1)S(1)}, bf16[32,2048]{1,0:T(8,128)(2,1)S(1)}, u32[]{:S(2)}, u32[]{:S(2)}) %collective-permute-start.1) | collective-permute-done | bytes 131104 | tf_op jit(solution)/shard_map/ppermute | solution.py:17
  15.5 7.1 %collective-permute-done.2 = bf16[32,2048]{1,0:T(8,128)(2,1)S(1)} collective-permute-done((bf16[32,2048]{1,0:T(8,128)(2,1)S(1)}, bf16[32,2048]{1,0:T(8,128)(2,1)S(1)}, u32[]{:S(2)}, u32[]{:S(2)}) %collective-permute-start.2) | collective-permute-done | bytes 131104 | tf_op jit(solution)/shard_map/ppermute | solution.py:17
  22.6 0.0 collective-permute-start.3
  22.6 7.1 %collective-permute-done.3 = bf16[32,2048]{1,0:T(8,128)(2,1)S(1)} collective-permute-done((bf16[32,2048]{1,0:T(8,128)(2,1)S(1)}, bf16[32,2048]{1,0:T(8,128)(2,1)S(1)}, u32[]{:S(2)}, u32[]{:S(2)}) %collective-permute-start.3) | collective-permute-done | bytes 131104 | tf_op jit(solution)/shard_map/ppermute | solution.py:17
  29.7 7.1 %collective-permute-done.4 = bf16[32,2048]{1,0:T(8,128)(2,1)S(1)} collective-permute-done((bf16[32,2048]{1,0:T(8,128)(2,1)S(1)}, bf16[32,2048]{1,0:T(8,128)(2,1)S(1)}, u32[]{:S(2)}, u32[]{:S(2)}) %collective-permute-start.4) | collective-permute-done | bytes 131104 | tf_op jit(solution)/shard_map/ppermute | solution.py:17
  36.8 7.1 %collective-permute-done.5 = bf16[32,2048]{1,0:T(8,128)(2,1)S(1)} collective-permute-done((bf16[32,2048]{1,0:T(8,128)(2,1)S(1)}, bf16[32,2048]{1,0:T(8,128)(2,1)S(1)}, u32[]{:S(2)}, u32[]{:S(2)}) %collective-permute-start.5) | collective-permute-done | bytes 131104 | tf_op jit(solution)/shard_map/ppermute | solution.py:17
  43.9 7.1 %collective-permute-done.6 = bf16[32,2048]{1,0:T(8,128)(2,1)S(1)} collective-permute-done((bf16[32,2048]{1,0:T(8,128)(2,1)S(1)}, bf16[32,2048]{1,0:T(8,128)(2,1)S(1)}, u32[]{:S(2)}, u32[]{:S(2)}) %collective-permute-start.6) | collective-permute-done | bytes 131104 | tf_op jit(solution)/shard_map/ppermute | solution.py:17
  51.0 7.1 %collective-permute-done.7 = bf16[32,2048]{1,0:T(8,128)(2,1)S(1)} collective-permute-done((bf16[32,2048]{1,0:T(8,128)(2,1)S(1)}, bf16[32,2048]{1,0:T(8,128)(2,1)S(1)}, u32[]{:S(2)}, u32[]{:S(2)}) %collective-permute-start.7) | collective-permute-done | bytes 131104 | tf_op jit(solution)/shard_map/ppermute | solution.py:17
  58.0 7.1 %collective-permute-done.8 = bf16[32,2048]{1,0:T(8,128)(2,1)S(1)} collective-permute-done((bf16[32,2048]{1,0:T(8,128)(2,1)S(1)}, bf16[32,2048]{1,0:T(8,128)(2,1)S(1)}, u32[]{:S(2)}, u32[]{:S(2)}) %collective-permute-start.8) | collective-permute-done | bytes 131104 | tf_op jit(solution)/shard_map/ppermute | solution.py:17
  65.1 7.1 %collective-permute-done.9 = bf16[32,2048]{1,0:T(8,128)(2,1)S(1)} collective-permute-done((bf16[32,2048]{1,0:T(8,128)(2,1)S(1)}, bf16[32,2048]{1,0:T(8,128)(2,1)S(1)}, u32[]{:S(2)}, u32[]{:S(2)}) %collective-permute-start.9) | collective-permute-done | bytes 131104 | tf_op jit(solution)/shard_map/ppermute | solution.py:17
  72.2 7.1 %collective-permute-done.10 = bf16[32,2048]{1,0:T(8,128)(2,1)S(1)} collective-permute-done((bf16[32,2048]{1,0:T(8,128)(2,1)S(1)}, bf16[32,2048]{1,0:T(8,128)(2,1)S(1)}, u32[]{:S(2)}, u32[]{:S(2)}) %collective-permute-start.10) | collective-permute-done | bytes 131104 | tf_op jit(solution)/shard_map/ppermute | solution.py:17
  79.3 7.1 %collective-permute-done.11 = bf16[32,2048]{1,0:T(8,128)(2,1)S(1)} collective-permute-done((bf16[32,2048]{1,0:T(8,128)(2,1)S(1)}, bf16[32,2048]{1,0:T(8,128)(2,1)S(1)}, u32[]{:S(2)}, u32[]{:S(2)}) %collective-permute-start.11) | collective-permute-done | bytes 131104 | tf_op jit(solution)/shard_map/ppermute | solution.py:17
  86.4 0.7 dynamic-slice_bitcast_fusion
  87.1 6.4 %collective-permute-done.12 = bf16[32,2048]{1,0:T(8,128)(2,1)S(1)} collective-permute-done((bf16[32,2048]{1,0:T(8,128)(2,1)S(1)}, bf16[32,2048]{1,0:T(8,128)(2,1)S(1)}, u32[]{:S(2)}, u32[]{:S(2)}) %collective-permute-start.12) | collective-permute-done | bytes 131104 | tf_op jit(solution)/shard_map/ppermute | solution.py:17
  93.5 0.8 fusion.13
  94.3 6.3 %collective-permute-done.13 = bf16[32,2048]{1,0:T(8,128)(2,1)S(1)} collective-permute-done((bf16[32,2048]{1,0:T(8,128)(2,1)S(1)}, bf16[32,2048]{1,0:T(8,128)(2,1)S(1)}, u32[]{:S(2)}, u32[]{:S(2)}) %collective-permute-start.13) | collective-permute-done | bytes 131104 | tf_op jit(solution)/shard_map/ppermute | solution.py:17
  100.6 0.7 exponential_convert_fusion
  101.3 1.0 copy.21
  102.3 1.0 copy.15
  103.3 4.6 %all-gather.1 = bf16[1,256,64]{1,2,0:T(8,128)(2,1)S(1)} all-gather(bf16[1,128,64]{1,2,0:T(8,128)(2,1)} %param.10), channel_id=3, replica_groups=mesh['fsdp'=16,'ctx'=2] {'ctx'}, dimensions={1}, use_global_device_ids=true | all-gather | bytes 49152 | tf_op jit(solution)/shard_map/all_gather | solution.py:59
  108.0 5.8 %all-gather = bf16[1,256,512]{2,1,0:T(8,128)(2,1)S(1)} all-gather(bf16[1,128,512]{2,1,0:T(8,128)(2,1)} %param.9), channel_id=2, replica_groups=mesh['fsdp'=16,'ctx'=2] {'ctx'}, dimensions={1}, use_global_device_ids=true | all-gather | bytes 393216 | tf_op jit(solution)/shard_map/all_gather | solution.py:58
  114.4 0.3 mul.24
  114.8 1.8 %convolution_convert_fusion = bf16[2048,256]{1,0:T(8,128)(2,1)S(1)} fusion(bf16[64,8,16,128]{3,2,1,0:T(8,128)(2,1)S(1)} %bitcast.38, bf16[1024,2048]{1,0:T(8,128)(2,1)S(1)} %constant_dynamic-update-slice_fusion, s32[]{:T(128)S(6)} %select_n.21, bf16[1,256,512]{2,1,0:T(8,128)(2,1)S(1)} %all-gather), kind=kOutput, calls=%fused_computation.1 | convolution fusion | flops 541589504 | bytes 5505028 | tf_op jit(solution)/shard_map/dot_general | solution.py:63
  116.6 0.3 convolution_bitcast_fusion.1
  116.9 0.3 fusion.7
  117.3 0.2 fusion.17
  117.5 1.0 abs_reduce_fusion
  118.6 37.0 %pmax.7 = f32[]{:T(128)} all-reduce(f32[]{:T(128)} %get-tuple-element.5), channel_id=1, replica_groups=mesh['fsdp'=16,'ctx'=2] {'fsdp','ctx'}, use_global_device_ids=true, to_apply=%region_3.4 | all-reduce | flops 1 | bytes 8 | tf_op jit(solution)/shard_map/pmax | solution.py:73
  155.6 0.7 divide_convert_fusion.1
  156.3 0.9 copy.17
  (49 shorter events, 0.4 us)
Async XLA Ops:
  0.0 114.1 %copy-start = (bf16[32,2048]{1,0:T(8,128)(2,1)S(1)}, bf16[32,2048]{1,0:T(8,128)(2,1)}, u32[]{:S(2)}) copy-start(bf16[32,2048]{1,0:T(8,128)(2,1)} %param.11) | copy-start | bytes 393220
  0.0 8.4 %collective-permute-start = (bf16[32,2048]{1,0:T(8,128)(2,1)}, bf16[32,2048]{1,0:T(8,128)(2,1)S(1)}, u32[]{:S(2)}, u32[]{:S(2)}) collective-permute-start(bf16[32,2048]{1,0:T(8,128)(2,1)} %param.11), channel_id=1, source_target_pairs={{0,2},{2,4},{4,6},{6,8},{8,10},{10,12},{12,14},{14,16},{16,18},{18... | collective-permute-start | bytes 393224 | tf_op jit(solution)/shard_map/ppermute | solution.py:17
  8.4 7.1 %collective-permute-start.1 = (bf16[32,2048]{1,0:T(8,128)(2,1)S(1)}, bf16[32,2048]{1,0:T(8,128)(2,1)S(1)}, u32[]{:S(2)}, u32[]{:S(2)}) collective-permute-start(bf16[32,2048]{1,0:T(8,128)(2,1)S(1)} %collective-permute-done), channel_id=1, source_target_pairs={{0,2},{2,4},{4,6},{6,8},{8,10},{10,12},{12,14},{14,16},{16,18},{18... | collective-permute-start | bytes 393224 | tf_op jit(solution)/shard_map/ppermute | solution.py:17
  15.5 7.1 %collective-permute-start.2 = (bf16[32,2048]{1,0:T(8,128)(2,1)S(1)}, bf16[32,2048]{1,0:T(8,128)(2,1)S(1)}, u32[]{:S(2)}, u32[]{:S(2)}) collective-permute-start(bf16[32,2048]{1,0:T(8,128)(2,1)S(1)} %collective-permute-done.1), channel_id=1, source_target_pairs={{0,2},{2,4},{4,6},{6,8},{8,10},{10,12},{12,14},{14,16},{16,18},{18... | collective-permute-start | bytes 393224 | tf_op jit(solution)/shard_map/ppermute | solution.py:17
  22.6 7.1 %collective-permute-start.3 = (bf16[32,2048]{1,0:T(8,128)(2,1)S(1)}, bf16[32,2048]{1,0:T(8,128)(2,1)S(1)}, u32[]{:S(2)}, u32[]{:S(2)}) collective-permute-start(bf16[32,2048]{1,0:T(8,128)(2,1)S(1)} %collective-permute-done.2), channel_id=1, source_target_pairs={{0,2},{2,4},{4,6},{6,8},{8,10},{10,12},{12,14},{14,16},{16,18},{18... | collective-permute-start | bytes 393224 | tf_op jit(solution)/shard_map/ppermute | solution.py:17
  29.7 7.1 %collective-permute-start.4 = (bf16[32,2048]{1,0:T(8,128)(2,1)S(1)}, bf16[32,2048]{1,0:T(8,128)(2,1)S(1)}, u32[]{:S(2)}, u32[]{:S(2)}) collective-permute-start(bf16[32,2048]{1,0:T(8,128)(2,1)S(1)} %collective-permute-done.3), channel_id=1, source_target_pairs={{0,2},{2,4},{4,6},{6,8},{8,10},{10,12},{12,14},{14,16},{16,18},{18... | collective-permute-start | bytes 393224 | tf_op jit(solution)/shard_map/ppermute | solution.py:17
  36.8 7.1 %collective-permute-start.5 = (bf16[32,2048]{1,0:T(8,128)(2,1)S(1)}, bf16[32,2048]{1,0:T(8,128)(2,1)S(1)}, u32[]{:S(2)}, u32[]{:S(2)}) collective-permute-start(bf16[32,2048]{1,0:T(8,128)(2,1)S(1)} %collective-permute-done.4), channel_id=1, source_target_pairs={{0,2},{2,4},{4,6},{6,8},{8,10},{10,12},{12,14},{14,16},{16,18},{18... | collective-permute-start | bytes 393224 | tf_op jit(solution)/shard_map/ppermute | solution.py:17
  43.9 7.1 %collective-permute-start.6 = (bf16[32,2048]{1,0:T(8,128)(2,1)S(1)}, bf16[32,2048]{1,0:T(8,128)(2,1)S(1)}, u32[]{:S(2)}, u32[]{:S(2)}) collective-permute-start(bf16[32,2048]{1,0:T(8,128)(2,1)S(1)} %collective-permute-done.5), channel_id=1, source_target_pairs={{0,2},{2,4},{4,6},{6,8},{8,10},{10,12},{12,14},{14,16},{16,18},{18... | collective-permute-start | bytes 393224 | tf_op jit(solution)/shard_map/ppermute | solution.py:17
  51.0 7.1 %collective-permute-start.7 = (bf16[32,2048]{1,0:T(8,128)(2,1)S(1)}, bf16[32,2048]{1,0:T(8,128)(2,1)S(1)}, u32[]{:S(2)}, u32[]{:S(2)}) collective-permute-start(bf16[32,2048]{1,0:T(8,128)(2,1)S(1)} %collective-permute-done.6), channel_id=1, source_target_pairs={{0,2},{2,4},{4,6},{6,8},{8,10},{10,12},{12,14},{14,16},{16,18},{18... | collective-permute-start | bytes 393224 | tf_op jit(solution)/shard_map/ppermute | solution.py:17
  58.0 7.1 %collective-permute-start.8 = (bf16[32,2048]{1,0:T(8,128)(2,1)S(1)}, bf16[32,2048]{1,0:T(8,128)(2,1)S(1)}, u32[]{:S(2)}, u32[]{:S(2)}) collective-permute-start(bf16[32,2048]{1,0:T(8,128)(2,1)S(1)} %collective-permute-done.7), channel_id=1, source_target_pairs={{0,2},{2,4},{4,6},{6,8},{8,10},{10,12},{12,14},{14,16},{16,18},{18... | collective-permute-start | bytes 393224 | tf_op jit(solution)/shard_map/ppermute | solution.py:17
  65.1 7.1 %collective-permute-start.9 = (bf16[32,2048]{1,0:T(8,128)(2,1)S(1)}, bf16[32,2048]{1,0:T(8,128)(2,1)S(1)}, u32[]{:S(2)}, u32[]{:S(2)}) collective-permute-start(bf16[32,2048]{1,0:T(8,128)(2,1)S(1)} %collective-permute-done.8), channel_id=1, source_target_pairs={{0,2},{2,4},{4,6},{6,8},{8,10},{10,12},{12,14},{14,16},{16,18},{18... | collective-permute-start | bytes 393224 | tf_op jit(solution)/shard_map/ppermute | solution.py:17
  72.2 7.1 %collective-permute-start.10 = (bf16[32,2048]{1,0:T(8,128)(2,1)S(1)}, bf16[32,2048]{1,0:T(8,128)(2,1)S(1)}, u32[]{:S(2)}, u32[]{:S(2)}) collective-permute-start(bf16[32,2048]{1,0:T(8,128)(2,1)S(1)} %collective-permute-done.9), channel_id=1, source_target_pairs={{0,2},{2,4},{4,6},{6,8},{8,10},{10,12},{12,14},{14,16},{16,18},{18... | collective-permute-start | bytes 393224 | tf_op jit(solution)/shard_map/ppermute | solution.py:17
  79.3 7.1 %collective-permute-start.11 = (bf16[32,2048]{1,0:T(8,128)(2,1)S(1)}, bf16[32,2048]{1,0:T(8,128)(2,1)S(1)}, u32[]{:S(2)}, u32[]{:S(2)}) collective-permute-start(bf16[32,2048]{1,0:T(8,128)(2,1)S(1)} %collective-permute-done.10), channel_id=1, source_target_pairs={{0,2},{2,4},{4,6},{6,8},{8,10},{10,12},{12,14},{14,16},{16,18},{18... | collective-permute-start | bytes 393224 | tf_op jit(solution)/shard_map/ppermute | solution.py:17
  86.4 7.1 %collective-permute-start.12 = (bf16[32,2048]{1,0:T(8,128)(2,1)S(1)}, bf16[32,2048]{1,0:T(8,128)(2,1)S(1)}, u32[]{:S(2)}, u32[]{:S(2)}) collective-permute-start(bf16[32,2048]{1,0:T(8,128)(2,1)S(1)} %collective-permute-done.11), channel_id=1, source_target_pairs={{0,2},{2,4},{4,6},{6,8},{8,10},{10,12},{12,14},{14,16},{16,18},{18... | collective-permute-start | bytes 393224 | tf_op jit(solution)/shard_map/ppermute | solution.py:17
  93.5 7.1 %collective-permute-start.13 = (bf16[32,2048]{1,0:T(8,128)(2,1)S(1)}, bf16[32,2048]{1,0:T(8,128)(2,1)S(1)}, u32[]{:S(2)}, u32[]{:S(2)}) collective-permute-start(bf16[32,2048]{1,0:T(8,128)(2,1)S(1)} %collective-permute-done.12), channel_id=1, source_target_pairs={{0,2},{2,4},{4,6},{6,8},{8,10},{10,12},{12,14},{14,16},{16,18},{18... | collective-permute-start | bytes 393224 | tf_op jit(solution)/shard_map/ppermute | solution.py:17
  100.6 13.2 %collective-permute-start.14 = (bf16[32,2048]{1,0:T(8,128)(2,1)S(1)}, bf16[32,2048]{1,0:T(8,128)(2,1)S(1)}, u32[]{:S(2)}, u32[]{:S(2)}) collective-permute-start(bf16[32,2048]{1,0:T(8,128)(2,1)S(1)} %collective-permute-done.13), channel_id=1, source_target_pairs={{0,2},{2,4},{4,6},{6,8},{8,10},{10,12},{12,14},{14,16},{16,18},{18... | collective-permute-start | bytes 393224 | tf_op jit(solution)/shard_map/ppermute | solution.py:17
